TPU v7x, 32 devices: a whole 2x2x4 slice. The times are simulated.
32 devices in a mesh: row: 8 (over y, x, core), ctx: 4 (over z).
Axes of the slice: x: 2, y: 2, z: 4, core: 2. Of those that a mesh axis runs over, the one named last changes fastest.
Arguments:
- queries: bfloat16 [5, 4096, 128], P(None, ('row', 'ctx')), may hold values from -100 to 100
- keys: bfloat16 [4096, 128], P('ctx'), may hold values from -6 to 6
- doc_ids: int32 [64], replicated, may hold values from 0 to 3, never falling along the last dimension, each value on 1 to 48 neighbouring positions
- gate_query: bfloat16 [5, 128, 128], replicated, may hold values from -0.5 to 0.5
- gate_key: bfloat16 [384, 128], replicated, may hold values from -0.3125 to 0.3125
Outputs:
- block_map: float32 [5, 64, 64], P(None, ('row', 'ctx'))
- grad_query: float32 [5, 128, 128], replicated
- grad_key: float32 [384, 128], replicated
Inputs may be any that keep to these rules, and one draw needn't show every extreme that they name: `doc_ids`: block document ids never fall along the sequence; each document spans 1 to 48 blocks and one spans exactly 48.
All inputs are finite; a program needn't handle non-finite values.
Results may differ from a plain program's by a relative error of at most 0.0003.
Values may be sent and summed in bfloat16 or wider, within the bound.
A program may use at most 64 MiB of HBM per device.

v0:
```python
import functools
import math

import jax
import jax.numpy as jnp
from jax import lax
from jax.experimental import pallas as pl
from jax.experimental.pallas import tpu as pltpu
from jax.sharding import PartitionSpec as P

BLK = 64
NEG = -1e30
PIECE = 16
GROUP = 4
MESH = pl.DeviceIdType.MESH
HI = lax.Precision.HIGHEST


def fdot(a, b, dims):
    return lax.dot_general(a, b, (dims, ((), ())), precision=HI, preferred_element_type=jnp.float32)


def kernel(
    R, C, q_ref, k_ref, doc_ref, gq_ref, gk_ref,
    bm_ref, qp_ref, qg_ref, both_ref, pooled_ref, diff_ref,
    kbuf, q_t, peak, bsum, pieces, diff_own, diff_all,
    s1, s2, s3, rsem, ps1, ps2, ps3, pctx, prow, ds1, ds2, dctx, drow,
):
    H, rows, D = q_ref.shape
    shard = k_ref.shape[0]
    nb = rows // BLK
    n = R * C
    TB = n * nb
    r = lax.axis_index("row")
    c = lax.axis_index("ctx")
    me = r * C + c
    half = R // 2
    scale = 1.0 / math.sqrt(D)
    used = H * nb

    def ctx_peer(d):
        return lax.rem(c + d, C)

    def row_peer(d):
        return lax.rem(r + 2 * d, R)

    partner = r + 1 - 2 * lax.rem(r, 2)

    def other_row(e):
        return lax.rem(partner + 2 * e, R)

    def needs(rr, cc):
        return cc * R < (rr // 2 + 1) * 2 * C

    barrier = pltpu.get_barrier_semaphore()
    for d in range(1, C):
        pl.semaphore_signal(barrier, inc=1, device_id=(r, ctx_peer(d)), device_id_type=MESH)
    for d in range(1, half):
        pl.semaphore_signal(barrier, inc=1, device_id=(row_peer(d), c), device_id_type=MESH)
    pl.semaphore_signal(barrier, inc=1, device_id=(partner, c), device_id_type=MESH)

    def slot(cc, rr):
        return pl.ds(pl.multiple_of(cc * shard + rr * rows, rows), rows)

    def part(rr):
        return pl.ds(pl.multiple_of(rr * PIECE, PIECE), PIECE)

    for h in range(H):
        qf = q_ref[h].astype(jnp.float32)
        q_t[:, h * rows:(h + 1) * rows] = qf.T.astype(jnp.bfloat16)
        for j in range(nb):
            pieces[c, pl.ds(r * PIECE + h * nb + j, 1), :] = jnp.mean(
                qf[j * BLK:(j + 1) * BLK], axis=0, keepdims=True
            )
    wide = k_ref[pl.ds(pl.multiple_of(r * rows, rows), rows), :].astype(jnp.float32)
    for j in range(nb):
        t = wide[j * BLK:(j + 1) * BLK]
        for i, pool in enumerate((jnp.max, jnp.min, jnp.mean)):
            pieces[c, pl.ds(r * PIECE + used + i * nb + j, 1), :] = pool(
                t, axis=0, keepdims=True
            )
    peak[...] = jnp.full_like(peak, NEG)
    bsum[...] = jnp.zeros_like(bsum)

    a0 = me * nb
    lane = lax.broadcasted_iota(jnp.int32, (1, rows), 1)
    qdoc = jnp.zeros((1, rows), jnp.int32)
    for j in range(nb):
        qdoc = jnp.where(lane // BLK == j, doc_ref[a0 + j], qdoc)

    def score(num, keys, diagonal):
        for h in range(H):
            s = jnp.dot(
                keys, q_t[:, h * rows:(h + 1) * rows], preferred_element_type=jnp.float32
            )
            if diagonal:
                ki = lax.broadcasted_iota(jnp.int32, (rows, rows), 0)
                qi = lax.broadcasted_iota(jnp.int32, (rows, rows), 1)
                s = jnp.where(ki <= qi, s, NEG)
            for j in range(keys.shape[0] // BLK):
                b = num * nb + j
                t = s[j * BLK:(j + 1) * BLK]
                top = jnp.max(t, axis=0, keepdims=True)
                total = jnp.sum(
                    jnp.exp2((t - top) * (scale * math.log2(math.e))), axis=0, keepdims=True
                )
                peak[h, pl.ds(b, 1), :] = jnp.where(qdoc == doc_ref[b], top * scale, NEG)
                bsum[h, pl.ds(b, 1), :] = total

    group = math.gcd(R, GROUP)

    def process(ref, base, first):
        @pl.when(first + group <= me)
        def _():
            for i in range(0, group, 2):
                at = pl.multiple_of(base + i * rows, rows)
                score(first + i, ref[pl.ds(at, 2 * rows), :], False)

        @pl.when(first + group > me)
        def _():
            @pl.loop(0, group)
            def _(i):
                at = pl.ds(pl.multiple_of(base + i * rows, rows), rows)

                @pl.when(first + i < me)
                def _():
                    score(first + i, ref[at, :], False)

                @pl.when(first + i == me)
                def _():
                    score(first + i, ref[at, :], True)

    @pl.loop(0, R // group)
    def _(g):
        process(k_ref, g * group * rows, c * R + g * group)

    pl.semaphore_wait(barrier, C - 1 + half)

    def copy1(d):
        return pltpu.make_async_remote_copy(
            src_ref=k_ref.at[pl.ds(pl.multiple_of(r * rows, rows), rows)],
            dst_ref=kbuf.at[slot(c, r)],
            send_sem=s1.at[d], recv_sem=rsem.at[c * R + r],
            device_id=(r, ctx_peer(d)), device_id_type=MESH,
        )

    def copy2(d, e):
        cc = ctx_peer(d)
        return pltpu.make_async_remote_copy(
            src_ref=kbuf.at[slot(cc, r)], dst_ref=kbuf.at[slot(cc, r)],
            send_sem=s2.at[d * half + e], recv_sem=rsem.at[cc * R + r],
            device_id=(row_peer(e), c), device_id_type=MESH,
        )

    def copy3(d, e):
        cc, rr = ctx_peer(d), row_peer(e)
        return pltpu.make_async_remote_copy(
            src_ref=kbuf.at[slot(cc, rr)], dst_ref=kbuf.at[slot(cc, rr)],
            send_sem=s3.at[d * half + e], recv_sem=rsem.at[cc * R + rr],
            device_id=(partner, c), device_id_type=MESH,
        )

    def arrived(cc, rr):
        pltpu.make_async_copy(
            kbuf.at[slot(cc, rr)], kbuf.at[slot(cc, rr)], rsem.at[cc * R + rr]
        ).wait()

    def piece1(d):
        return pltpu.make_async_remote_copy(
            src_ref=pieces.at[c, part(r)], dst_ref=pieces.at[c, part(r)],
            send_sem=ps1.at[d], recv_sem=pctx.at[c],
            device_id=(r, ctx_peer(d)), device_id_type=MESH,
        )

    def piece2(e):
        return pltpu.make_async_remote_copy(
            src_ref=pieces.at[:, part(r)], dst_ref=pieces.at[:, part(r)],
            send_sem=ps2.at[e], recv_sem=prow.at[r],
            device_id=(row_peer(e), c), device_id_type=MESH,
        )

    def piece3(e):
        rr = row_peer(e)
        return pltpu.make_async_remote_copy(
            src_ref=pieces.at[:, part(rr)], dst_ref=pieces.at[:, part(rr)],
            send_sem=ps3.at[e], recv_sem=prow.at[rr],
            device_id=(partner, c), device_id_type=MESH,
        )

    def row_arrived(rr):
        pltpu.make_async_copy(
            pieces.at[:, part(rr)], pieces.at[:, part(rr)], prow.at[rr]
        ).wait()

    for d in range(1, C):
        piece1(d).start()
    for d in range(1, C):
        copy1(d).start()

    for d in range(1, C):
        cc = ctx_peer(d)
        pltpu.make_async_copy(pieces.at[cc, part(r)], pieces.at[cc, part(r)], pctx.at[cc]).wait()
    for e in range(1, half):
        piece2(e).start()
    piece3(0).start()

    for d in range(1, C):
        cc = ctx_peer(d)
        arrived(cc, r)
        for e in range(1, half):
            @pl.when(needs(row_peer(e), cc))
            def _():
                copy2(d, e).start()

        @pl.when(needs(r, cc))
        def _():
            copy3(d, 0).start()

    for e in range(1, half):
        row_arrived(row_peer(e))
        piece3(e).start()

    @pl.loop(1, C)
    def _(d):
        @pl.when(needs(r, ctx_peer(d)))
        def _():
            @pl.loop(1, half)
            def _(e):
                arrived(ctx_peer(d), row_peer(e))
                copy3(d, e).start()

    for e in range(half):
        row_arrived(other_row(e))

    def gathered(j):
        return jnp.concatenate(
            [pieces[i, pl.ds(j, R, stride=PIECE), :] for i in range(C)], axis=0
        )

    lanes_k = []
    for i in range(3):
        halves = [gathered(used + i * nb + j) for j in range(nb)]
        lanes_k.append(jnp.stack(halves, axis=1).reshape(TB, D))
    pooled = jnp.concatenate(lanes_k, axis=1)
    key_gate = fdot(pooled, gk_ref[...].astype(jnp.float32), ((1,), (0,)))
    row16 = lax.broadcasted_iota(jnp.int32, (PIECE, 1), 0)
    own = pieces[c, part(r), :]
    qg = jnp.zeros((PIECE, D), jnp.float32)
    for h in range(H):
        gate = gq_ref[h].astype(jnp.float32)
        qg = jnp.where(row16 // nb == h, fdot(own, gate, ((1,), (0,))), qg)
    logits = fdot(qg, key_gate, ((1,), (1,)))

    @pl.loop(1, C)
    def _(d):
        cc = ctx_peer(d)

        @pl.when(needs(r, cc))
        def _():
            @pl.loop(0, half)
            def _(e):
                arrived(cc, other_row(e))

            @pl.loop(0, R // group)
            def _(g):
                process(kbuf, cc * shard + g * group * rows, cc * R + g * group)

    maps = jnp.full((PIECE, TB), NEG, jnp.float32)
    for h in range(H):
        pk = peak[h]
        top = jnp.max(pk, axis=0, keepdims=True)
        total = jnp.sum(bsum[h] * jnp.exp(pk - top), axis=0, keepdims=True)
        chance = (pk - (top + jnp.log(total))).T
        for j in range(nb):
            best = jnp.max(chance[j * BLK:(j + 1) * BLK], axis=0, keepdims=True)
            maps = jnp.where(row16 == h * nb + j, best, maps)
    allowed = maps > 0.01 * NEG
    block_map = jnp.where(allowed, jnp.exp(maps), 0.0)
    live = row16 < used
    gate_exp = jnp.where(allowed, jnp.exp(logits), 0.0)
    gate_sum = jnp.where(live, jnp.sum(gate_exp, axis=1, keepdims=True), 1.0)
    map_sum = jnp.where(live, jnp.sum(block_map, axis=1, keepdims=True), 1.0)
    diff = gate_exp / gate_sum - block_map / map_sum
    for h in range(H):
        for j in range(nb):
            diff_own[h:h + 1, j * TB:(j + 1) * TB] = diff[h * nb + j:h * nb + j + 1, :]

    def send(d, e):
        to_row, to_ctx = r + e, c + d
        to_row = jnp.where(to_row >= R, to_row - R, to_row)
        to_ctx = jnp.where(to_ctx >= C, to_ctx - C, to_ctx)
        return pltpu.make_async_remote_copy(
            src_ref=diff_own, dst_ref=diff_all.at[c * R + r],
            send_sem=ds1.at[0], recv_sem=dctx.at[0],
            device_id=(to_row, to_ctx), device_id_type=MESH,
        )

    for e in range(R - 1, -1, -1):
        for d in range(C - 1, -1, -1):
            if d or e:
                send(d, e).start()
    diff_all[c * R + r] = diff_own[...]
    for h in range(H):
        for j in range(nb):
            bm_ref[h, j:j + 1, :] = block_map[h * nb + j:h * nb + j + 1, :]


    for h in range(H):
        qp = jnp.concatenate([gathered(h * nb + j) for j in range(nb)], axis=0)
        qp_ref[h] = qp
        qg_ref[h] = fdot(qp, gq_ref[h].astype(jnp.float32), ((1,), (0,)))

    for j in range(nb):
        both_ref[j * TB:(j + 1) * TB] = key_gate
    pooled_ref[...] = pooled
    rest = diff_all.at[pl.ds(0, n - 1)]
    pltpu.make_async_copy(rest, rest, dctx.at[0]).wait()
    diff_ref[...] = diff_all[...]
    pltpu.make_async_copy(rest, rest, ds1.at[0]).wait()
    for d in range(1, C):
        cc = ctx_peer(d)
        copy1(d).wait_send()
        piece1(d).wait_send()
        for e in range(half):
            @pl.when(needs(r, cc))
            def _():
                copy3(d, e).wait_send()

            if e > 0:
                @pl.when(needs(row_peer(e), cc))
                def _():
                    copy2(d, e).wait_send()
    for e in range(half):
        piece3(e).wait_send()
        if e > 0:
            piece2(e).wait_send()


def finish(map_ref, qp_ref, qg_ref, both_ref, pooled_ref, diff_ref, bm_ref, dq_ref, dk_ref):
    H, nb, TB = map_ref.shape
    bm_ref[...] = map_ref[...]
    both = both_ref[...]
    wide_lane = lax.broadcasted_iota(jnp.int32, (1, nb * TB), 1)
    key_back = jnp.zeros(both.shape, jnp.float32)
    for h in range(H):
        mixed = diff_ref[:, h, :]
        diff = jnp.concatenate(
            [jnp.where(wide_lane // TB == j, mixed, 0.0) for j in range(nb)], axis=0
        )
        back = fdot(diff, both, ((1,), (0,)))
        dq_ref[h] = fdot(qp_ref[h], back, ((0,), (0,)))
        key_back = key_back + fdot(diff, qg_ref[h], ((0,), (0,)))
    folded = key_back[:TB]
    for j in range(1, nb):
        folded = folded + key_back[j * TB:(j + 1) * TB]
    dk_ref[...] = fdot(pooled_ref[...], folded, ((0,), (0,)))


def shards(R, C, queries, keys, doc_ids, gate_query, gate_key):
    H, rows, D = queries.shape
    n = R * C
    nb = rows // BLK
    TB = doc_ids.shape[0]
    half = R // 2
    vm = pl.BlockSpec(memory_space=pltpu.VMEM)
    sm = pl.BlockSpec(memory_space=pltpu.SMEM)
    dma = pltpu.SemaphoreType.DMA
    parts = pl.pallas_call(
        functools.partial(kernel, R, C),
        out_shape=(
            jax.ShapeDtypeStruct((H, nb, TB), jnp.float32),
            jax.ShapeDtypeStruct((H, nb * n, D), jnp.float32),
            jax.ShapeDtypeStruct((H, nb * n, D), jnp.float32),
            jax.ShapeDtypeStruct((nb * TB, D), jnp.float32),
            jax.ShapeDtypeStruct((TB, 3 * D), jnp.float32),
            jax.ShapeDtypeStruct((n, H, nb * TB), jnp.float32),
        ),
        in_specs=[vm, vm, sm, vm, vm],
        out_specs=(vm,) * 6,
        scratch_shapes=[
            pltpu.VMEM((C * keys.shape[0], D), jnp.bfloat16),
            pltpu.VMEM((D, H * rows), jnp.bfloat16),
            pltpu.VMEM((H, TB, rows), jnp.float32),
            pltpu.VMEM((H, TB, rows), jnp.float32),
            pltpu.VMEM((C, R * PIECE, D), jnp.float32),
            pltpu.VMEM((H, nb * TB), jnp.float32),
            pltpu.VMEM((n, H, nb * TB), jnp.float32),
            dma((C,)), dma((C * half,)), dma((C * half,)), dma((n,)),
            dma((C,)), dma((half,)), dma((half,)), dma((C,)), dma((R,)),
            dma((C,)), dma((R,)), dma((C,)), dma((R,)),
        ],
        compiler_params=pltpu.CompilerParams(
            collective_id=0, has_side_effects=True, vmem_limit_bytes=60 * 1024 * 1024
        ),
    )(queries, keys, doc_ids, gate_query, gate_key)
    return pl.pallas_call(
        finish,
        out_shape=(
            jax.ShapeDtypeStruct((H, nb, TB), jnp.float32),
            jax.ShapeDtypeStruct(gate_query.shape, jnp.float32),
            jax.ShapeDtypeStruct(gate_key.shape, jnp.float32),
        ),
        in_specs=[vm] * 6,
        out_specs=(vm,) * 3,
        compiler_params=pltpu.CompilerParams(vmem_limit_bytes=60 * 1024 * 1024),
    )(*parts)


def solution(mesh):
    R, C = mesh.shape["row"], mesh.shape["ctx"]
    in_specs = (P(None, ("row", "ctx"), None), P("ctx", None), P(), P(), P())
    out_specs = (P(None, ("row", "ctx"), None), P(), P())
    return jax.shard_map(
        functools.partial(shards, R, C), mesh=mesh, in_specs=in_specs, out_specs=out_specs,
        check_vma=False,
    )
```

profile of v0, /device:TPU:0, one launch (start us, length us, event | category | flops | bytes accessed | tf_op | source)
XLA Modules:
  0.0 33.1 jit_solution(11479078225816048906)
XLA Ops:
  0.6 28.4 %shard_map.76 = (f32[5,2,64]{2,1,0:T(2,128)}, f32[5,64,128]{2,1,0:T(8,128)}, f32[5,64,128]{2,1,0:T(8,128)}, f32[128,128]{1,0:T(8,128)}, f32[64,384]{1,0:T(8,128)}, /*index=5*/f32[32,5,128]{2,1,0:T(8,128)}) custom-call(bf16[5,128,128]{2,1,0:T(8,128)(2,1)} %q_ref.1, bf16[1024,128]{1,0:T(8,128)(2,1)} %k_ref.1, s32[64]{0:T(128)} %doc_ref.1, ...), custom_call_target="tpu_custom_call" | custom-call | tf_op jit(solution)/shard_map/pallas_call | solution.py:368
  29.1 4.0 %shard_map.77 = (f32[5,2,64]{2,1,0:T(2,128)}, f32[5,128,128]{2,1,0:T(8,128)}, f32[384,128]{1,0:T(8,128)}) custom-call(f32[5,2,64]{2,1,0:T(2,128)} %get-tuple-element.9.map_ref, f32[5,64,128]{2,1,0:T(8,128)} %get-tuple-element.10.qp_ref, f32[5,64,128]{2,1,0:T(8,128)} %get-tuple-element.11.qg_ref, f32[128,128]{1,0:T(8,128)} %get-tuple-element.12.both_ref, ...), custom_call_target="tpu_custom_call" | custom-call | tf_op jit(solution)/shard_map/pallas_call | solution.py:396
where the time goes:
time: 33.2 us; the launch traced here: 33.1 us
  Pallas kernels  32.4 us (98%)
  between operations  0.64 us (2%)
    pallas_call x1, Pallas kernels, shards(): pl.pallas_call(functools.partial(kernel, R, C), out_shape=(jax.ShapeDtype...  28.4 us
    pallas_call x1, Pallas kernels, shards(): pl.pallas_call(finish, out_shape=(jax.ShapeDtypeStruct((H, nb, TB), jnp.f...  3.99 us

commit v1 on v0

v1 whole, which is shorter than its diff:
```python
import functools
import math

import jax
import jax.numpy as jnp
from jax import lax
from jax.experimental import pallas as pl
from jax.experimental.pallas import tpu as pltpu
from jax.sharding import PartitionSpec as P

BLK = 64
NEG = -1e30
PIECE = 16
GROUP = 4
MOST = (3, 4)
MESH = pl.DeviceIdType.MESH
VMEM_LIMIT = 32 * 1024 * 1024
HI = lax.Precision.HIGHEST


def fdot(a, b, dims):
    return lax.dot_general(a, b, (dims, ((), ())), precision=HI, preferred_element_type=jnp.float32)


def gate(a, w):
    m = a.shape[0]
    hi = a.astype(jnp.bfloat16)
    rest = a - hi.astype(jnp.float32)
    mid = rest.astype(jnp.bfloat16)
    low = (rest - mid.astype(jnp.float32)).astype(jnp.bfloat16)
    p = jnp.dot(
        jnp.concatenate([hi, mid, low], axis=0), w, preferred_element_type=jnp.float32
    )
    return p[:m] + (p[m:2 * m] + p[2 * m:])


def kernel(
    R, C, q_hbm, k_hbm, doc_hbm, gq_hbm, gk_hbm,
    bm_ref, qp_ref, qg_ref, both_ref, pooled_ref, diff_ref,
    q_ref, gq_ref, gk_ref, doc_ref, kbuf, q_t, peak, bsum, kpool, pieces, diff_own, diff_all,
    local, keysent, rsem, ps1, ps2, ps3, pctx, prow, ds1, dctx,
):
    H, rows, D = q_ref.shape
    shard = R * rows
    nb = rows // BLK
    n = R * C
    TB = n * nb
    most = TB * MOST[0] // MOST[1]
    r = lax.axis_index("row")
    c = lax.axis_index("ctx")
    me = r * C + c
    half = R // 2
    scale = 1.0 / math.sqrt(D)
    used = H * nb
    cut = rows // 2

    def ctx_peer(d):
        return lax.rem(c + d, C)

    def flip(rr, e):
        bit = 2
        while e:
            if e % 2:
                rr = rr + bit - 2 * bit * lax.rem(rr // bit, 2)
            e, bit = e // 2, bit * 2
        return rr

    def row_peer(e):
        return flip(r, e)

    partner = r + 1 - 2 * lax.rem(r, 2)

    def other_row(e):
        return flip(partner, e)

    def others(i):
        return jnp.where(i >= c, i + 1, i)

    def far_first(i):
        down = C - 1 - i
        return jnp.where(2 * c < C, jnp.where(down <= c, down - 1, down), others(i))

    barrier = pltpu.get_barrier_semaphore()
    for d in range(1, C):
        pl.semaphore_signal(barrier, inc=1, device_id=(r, ctx_peer(d)), device_id_type=MESH)
    for e in range(1, half):
        pl.semaphore_signal(barrier, inc=1, device_id=(row_peer(e), c), device_id_type=MESH)
    pl.semaphore_signal(barrier, inc=1, device_id=(partner, c), device_id_type=MESH)

    def chunk(num):
        return pl.ds(pl.multiple_of(num * rows, rows), rows)

    def piece(num, x):
        return pl.ds(pl.multiple_of(num * rows + x * cut, cut), cut)

    def part(rr):
        return pl.ds(pl.multiple_of(rr * PIECE, PIECE), used)

    loads = [
        pltpu.make_async_copy(q_hbm, q_ref, local.at[0]),
        pltpu.make_async_copy(
            k_hbm, kbuf.at[pl.ds(pl.multiple_of(c * shard, shard), shard)], local.at[1]
        ),
        pltpu.make_async_copy(doc_hbm, doc_ref, local.at[2]),
        pltpu.make_async_copy(gq_hbm, gq_ref, local.at[3]),
        pltpu.make_async_copy(gk_hbm, gk_ref, local.at[4]),
    ]
    for load in loads:
        load.start()
    peak[...] = jnp.full_like(peak, NEG)
    bsum[...] = jnp.zeros_like(bsum)
    loads[0].wait()
    for h in range(H):
        qf = q_ref[h].astype(jnp.float32)
        q_t[:, h * rows:(h + 1) * rows] = qf.T.astype(jnp.bfloat16)
        for j in range(nb):
            pieces[c, pl.ds(r * PIECE + h * nb + j, 1), :] = jnp.mean(
                qf[j * BLK:(j + 1) * BLK], axis=0, keepdims=True
            )
    pl.semaphore_wait(barrier, C - 1 + half)

    def copy_ctx(cc):
        return pltpu.make_async_remote_copy(
            src_ref=k_hbm.at[pl.ds(pl.multiple_of(r * rows, rows), rows)],
            dst_ref=kbuf.at[chunk(c * R + r)],
            send_sem=keysent.at[0], recv_sem=rsem.at[c * R + r, 0],
            device_id=(r, cc), device_id_type=MESH,
        )

    def copy_whole(num, to):
        return pltpu.make_async_remote_copy(
            src_ref=kbuf.at[chunk(num)], dst_ref=kbuf.at[chunk(num)],
            send_sem=keysent.at[0], recv_sem=rsem.at[num, 0],
            device_id=(to, c), device_id_type=MESH,
        )

    def copy_half(num, x, to):
        return pltpu.make_async_remote_copy(
            src_ref=kbuf.at[piece(num, x)], dst_ref=kbuf.at[piece(num, x)],
            send_sem=keysent.at[0], recv_sem=rsem.at[num, x],
            device_id=(to, c), device_id_type=MESH,
        )

    def arrived(num):
        at = kbuf.at[chunk(num)]
        pltpu.make_async_copy(at, at, rsem.at[num, 0]).wait()

    def half_arrived(num, x):
        at = kbuf.at[piece(num, x)]
        pltpu.make_async_copy(at, at, rsem.at[num, x]).wait()

    def piece1(d):
        return pltpu.make_async_remote_copy(
            src_ref=pieces.at[c, part(r)], dst_ref=pieces.at[c, part(r)],
            send_sem=ps1.at[d], recv_sem=pctx.at[c],
            device_id=(r, ctx_peer(d)), device_id_type=MESH,
        )

    def piece2(e):
        return pltpu.make_async_remote_copy(
            src_ref=pieces.at[:, part(r)], dst_ref=pieces.at[:, part(r)],
            send_sem=ps2.at[e], recv_sem=prow.at[r],
            device_id=(row_peer(e), c), device_id_type=MESH,
        )

    def piece3(e):
        rr = row_peer(e)
        return pltpu.make_async_remote_copy(
            src_ref=pieces.at[:, part(rr)], dst_ref=pieces.at[:, part(rr)],
            send_sem=ps3.at[e], recv_sem=prow.at[rr],
            device_id=(partner, c), device_id_type=MESH,
        )

    def row_arrived(rr):
        pltpu.make_async_copy(
            pieces.at[:, part(rr)], pieces.at[:, part(rr)], prow.at[rr]
        ).wait()

    @pl.loop(0, C - 1)
    def _(i):
        copy_ctx(far_first(i)).start()

    for d in range(1, C):
        piece1(d).start()

    loads[2].wait()
    a0 = me * nb
    lane = lax.broadcasted_iota(jnp.int32, (1, 2 * rows), 1)
    qdoc = jnp.zeros((1, 2 * rows), jnp.int32)
    for j in range(nb):
        qdoc = jnp.where(lax.rem(lane, rows) // BLK == j, doc_ref[a0 + j], qdoc)

    def score(nums, masked):
        keys = jnp.concatenate([kbuf[chunk(num), :] for num in nums], axis=0)
        for h in range(0, H, 2):
            width = min(2, H - h) * rows
            cols = slice(h * rows, h * rows + width)
            s = jnp.dot(keys, q_t[:, cols], preferred_element_type=jnp.float32)
            if masked:
                ki = lax.broadcasted_iota(jnp.int32, s.shape, 0)
                qi = lax.rem(lax.broadcasted_iota(jnp.int32, s.shape, 1), rows)
                s = jnp.where(ki - qi <= (me - nums[0]) * rows, s, NEG)
            for m, num in enumerate(nums):
                for j in range(nb):
                    b = num * nb + j
                    at = (m * nb + j) * BLK
                    t = s[at:at + BLK]
                    top = jnp.max(t, axis=0, keepdims=True)
                    total = jnp.sum(
                        jnp.exp2((t - top) * (scale * math.log2(math.e))), axis=0, keepdims=True
                    )
                    top = jnp.where(qdoc[:, :width] == doc_ref[b], top * scale, NEG)
                    for k in range(width // rows):
                        peak[h + k, pl.ds(b, 1), :] = top[:, k * rows:(k + 1) * rows]
                        bsum[h + k, pl.ds(b, 1), :] = total[:, k * rows:(k + 1) * rows]

    def pool(num):
        wide = kbuf[chunk(num), :].astype(jnp.float32)
        for j in range(nb):
            t = wide[j * BLK:(j + 1) * BLK]
            for i, how in enumerate((jnp.max, jnp.min, jnp.mean)):
                kpool[i, pl.ds(num * nb + j, 1), :] = how(t, axis=0, keepdims=True)

    def near(num):
        return (num + 1) * nb - 1 + most > a0

    def process(nums):
        for num in nums:
            pool(num)
        whole = (nums[0] < me) & near(nums[0])
        for num in nums[1:]:
            whole = whole & (num < me) & near(num)

        @pl.when(whole)
        def _():
            for i in range(0, len(nums), 2):
                score(nums[i:i + 2], False)

        @pl.when(jnp.logical_not(whole))
        def _():
            for num in nums:
                @pl.when((num <= me) & near(num))
                def _():
                    score([num], True)

    loads[1].wait()

    @pl.loop(0, half)
    def _(g):
        process([c * R + 2 * g, c * R + 2 * g + 1])

    @pl.loop(0, C - 1)
    def _(i):
        num = others(i) * R + r
        arrived(num)
        copy_half(num, 0, row_peer(1)).start()
        copy_half(num, 1, row_peer(2)).start()
        copy_half(num, 1, row_peer(1)).start()
        copy_half(num, 0, row_peer(2)).start()
        for e in range(4, half):
            copy_whole(num, row_peer(e)).start()
        copy_whole(num, partner).start()

    @pl.loop(0, C - 1)
    def _(i):
        base = others(i) * R
        half_arrived(base + row_peer(1), 0)
        copy_half(base + row_peer(1), 0, row_peer(2)).start()
        half_arrived(base + row_peer(2), 1)
        copy_half(base + row_peer(2), 1, row_peer(1)).start()

    for d in range(1, C):
        cc = ctx_peer(d)
        pltpu.make_async_copy(pieces.at[cc, part(r)], pieces.at[cc, part(r)], pctx.at[cc]).wait()
    for e in range(1, half):
        piece2(e).start()
    piece3(0).start()

    @pl.loop(0, C - 1)
    def _(i):
        base = others(i) * R
        half_arrived(base + row_peer(1), 1)
        copy_whole(base + row_peer(1), partner).start()
        half_arrived(base + row_peer(2), 0)
        copy_whole(base + row_peer(2), partner).start()

    @pl.loop(0, C - 1)
    def _(i):
        base = others(i) * R
        arrived(base + partner)
        process([base + r, base + partner, base + row_peer(1), base + row_peer(2)])

    @pl.loop(0, C - 1)
    def _(i):
        num = others(i) * R + row_peer(3)
        half_arrived(num, 0)
        half_arrived(num, 1)
        copy_whole(num, partner).start()
        for e in range(4, half):
            arrived(others(i) * R + row_peer(e))
            copy_whole(others(i) * R + row_peer(e), partner).start()

    @pl.loop(0, C - 1)
    def _(i):
        base = others(i) * R
        arrived(base + other_row(1))
        arrived(base + other_row(2))
        process([base + row_peer(3), base + other_row(1), base + other_row(2)])

    for e in range(1, half):
        row_arrived(row_peer(e))
        piece3(e).start()

    @pl.loop(0, C - 1)
    def _(i):
        base = others(i) * R
        arrived(base + other_row(3))
        process([base + other_row(3)])
        for e in range(4, half):
            arrived(base + other_row(e))
            process([base + row_peer(e), base + other_row(e)])

    loads[3].wait()
    loads[4].wait()
    pooled = jnp.concatenate([kpool[i] for i in range(3)], axis=1)
    key_gate = gate(pooled, gk_ref[...])
    row16 = lax.broadcasted_iota(jnp.int32, (PIECE, 1), 0)
    own = jnp.where(row16 < used, pieces[c, pl.ds(pl.multiple_of(r * PIECE, PIECE), PIECE), :], 0.0)
    qg = jnp.zeros((PIECE, D), jnp.float32)
    for h in range(H):
        qg = jnp.where(row16 // nb == h, gate(own, gq_ref[h]), qg)
    logits = fdot(qg, key_gate, ((1,), (1,)))

    maps = jnp.full((PIECE, TB), NEG, jnp.float32)
    for h in range(H):
        pk = peak[h]
        top = jnp.max(pk, axis=0, keepdims=True)
        total = jnp.sum(bsum[h] * jnp.exp(pk - top), axis=0, keepdims=True)
        chance = (pk - (top + jnp.log(total))).T
        for j in range(nb):
            best = jnp.max(chance[j * BLK:(j + 1) * BLK], axis=0, keepdims=True)
            maps = jnp.where(row16 == h * nb + j, best, maps)
    allowed = maps > 0.01 * NEG
    block_map = jnp.where(allowed, jnp.exp(maps), 0.0)
    live = row16 < used
    gate_exp = jnp.where(allowed, jnp.exp(logits), 0.0)
    gate_sum = jnp.where(live, jnp.sum(gate_exp, axis=1, keepdims=True), 1.0)
    map_sum = jnp.where(live, jnp.sum(block_map, axis=1, keepdims=True), 1.0)
    diff = gate_exp / gate_sum - block_map / map_sum
    for h in range(H):
        for j in range(nb):
            diff_own[h:h + 1, j * TB:(j + 1) * TB] = diff[h * nb + j:h * nb + j + 1, :]

    def send(d, e):
        to_row, to_ctx = r + e, c + d
        to_row = jnp.where(to_row >= R, to_row - R, to_row)
        to_ctx = jnp.where(to_ctx >= C, to_ctx - C, to_ctx)
        return pltpu.make_async_remote_copy(
            src_ref=diff_own, dst_ref=diff_all.at[c * R + r],
            send_sem=ds1.at[0], recv_sem=dctx.at[0],
            device_id=(to_row, to_ctx), device_id_type=MESH,
        )

    for e in range(R - 1, -1, -1):
        for d in range(C - 1, -1, -1):
            if d or e:
                send(d, e).start()
    diff_all[c * R + r] = diff_own[...]
    for h in range(H):
        for j in range(nb):
            bm_ref[h, j:j + 1, :] = block_map[h * nb + j:h * nb + j + 1, :]

    for e in range(half):
        row_arrived(other_row(e))

    def gathered(j):
        return jnp.concatenate(
            [pieces[i, pl.ds(j, R, stride=PIECE), :] for i in range(C)], axis=0
        )

    for h in range(H):
        qp = jnp.concatenate([gathered(h * nb + j) for j in range(nb)], axis=0)
        qp_ref[h] = qp
        qg_ref[h] = gate(qp, gq_ref[h])

    for j in range(nb):
        both_ref[j * TB:(j + 1) * TB] = key_gate
    pooled_ref[...] = pooled
    rest = diff_all.at[pl.ds(0, n - 1)]
    pltpu.make_async_copy(rest, rest, dctx.at[0]).wait()
    diff_ref[...] = diff_all[...]
    pltpu.make_async_copy(rest, rest, ds1.at[0]).wait()
    sent = kbuf.at[pl.ds(0, (C - 1) * shard)]
    pltpu.make_async_copy(sent, sent, keysent.at[0]).wait()
    for d in range(1, C):
        piece1(d).wait_send()
    for e in range(half):
        piece3(e).wait_send()
        if e > 0:
            piece2(e).wait_send()


def finish(map_ref, qp_ref, qg_ref, both_ref, pooled_ref, diff_ref, bm_ref, dq_ref, dk_ref):
    H, nb, TB = map_ref.shape
    bm_ref[...] = map_ref[...]
    both = both_ref[...]
    wide_lane = lax.broadcasted_iota(jnp.int32, (1, nb * TB), 1)
    key_back = jnp.zeros(both.shape, jnp.float32)
    for h in range(H):
        mixed = diff_ref[:, h, :]
        diff = jnp.concatenate(
            [jnp.where(wide_lane // TB == j, mixed, 0.0) for j in range(nb)], axis=0
        )
        back = fdot(diff, both, ((1,), (0,)))
        dq_ref[h] = fdot(qp_ref[h], back, ((0,), (0,)))
        key_back = key_back + fdot(diff, qg_ref[h], ((0,), (0,)))
    folded = key_back[:TB]
    for j in range(1, nb):
        folded = folded + key_back[j * TB:(j + 1) * TB]
    dk_ref[...] = fdot(pooled_ref[...], folded, ((0,), (0,)))


def shards(R, C, queries, keys, doc_ids, gate_query, gate_key):
    H, rows, D = queries.shape
    n = R * C
    nb = rows // BLK
    TB = doc_ids.shape[0]
    half = R // 2
    vm = pl.BlockSpec(memory_space=pltpu.VMEM)
    hbm = pl.BlockSpec(memory_space=pltpu.HBM)
    dma = pltpu.SemaphoreType.DMA
    given = [
        pltpu.with_memory_space_constraint(x, pltpu.HBM)
        for x in (queries, keys, doc_ids, gate_query, gate_key)
    ]
    parts = pl.pallas_call(
        functools.partial(kernel, R, C),
        out_shape=(
            jax.ShapeDtypeStruct((H, nb, TB), jnp.float32),
            jax.ShapeDtypeStruct((H, nb * n, D), jnp.float32),
            jax.ShapeDtypeStruct((H, nb * n, D), jnp.float32),
            jax.ShapeDtypeStruct((nb * TB, D), jnp.float32),
            jax.ShapeDtypeStruct((TB, 3 * D), jnp.float32),
            jax.ShapeDtypeStruct((n, H, nb * TB), jnp.float32),
        ),
        in_specs=[hbm] * 5,
        out_specs=(vm,) * 6,
        scratch_shapes=[
            pltpu.VMEM(queries.shape, queries.dtype),
            pltpu.VMEM(gate_query.shape, gate_query.dtype),
            pltpu.VMEM(gate_key.shape, gate_key.dtype),
            pltpu.SMEM(doc_ids.shape, doc_ids.dtype),
            pltpu.VMEM((C * keys.shape[0], D), jnp.bfloat16),
            pltpu.VMEM((D, H * rows), jnp.bfloat16),
            pltpu.VMEM((H, TB, rows), jnp.float32),
            pltpu.VMEM((H, TB, rows), jnp.float32),
            pltpu.VMEM((3, TB, D), jnp.float32),
            pltpu.VMEM((C, R * PIECE, D), jnp.float32),
            pltpu.VMEM((H, nb * TB), jnp.float32),
            pltpu.VMEM((n, H, nb * TB), jnp.float32),
            dma((5,)), dma((1,)), dma((n, 2)),
            dma((C,)), dma((half,)), dma((half,)), dma((C,)), dma((R,)), dma((1,)), dma((1,)),
        ],
        compiler_params=pltpu.CompilerParams(
            collective_id=0, has_side_effects=True, vmem_limit_bytes=VMEM_LIMIT
        ),
    )(*given)
    return pl.pallas_call(
        finish,
        out_shape=(
            jax.ShapeDtypeStruct((H, nb, TB), jnp.float32),
            jax.ShapeDtypeStruct(gate_query.shape, jnp.float32),
            jax.ShapeDtypeStruct(gate_key.shape, jnp.float32),
        ),
        in_specs=[vm] * 6,
        out_specs=(vm,) * 3,
        compiler_params=pltpu.CompilerParams(vmem_limit_bytes=VMEM_LIMIT),
    )(*parts)


def solution(mesh):
    R, C = mesh.shape["row"], mesh.shape["ctx"]
    in_specs = (P(None, ("row", "ctx"), None), P("ctx", None), P(), P(), P())
    out_specs = (P(None, ("row", "ctx"), None), P(), P())
    return jax.shard_map(
        functools.partial(shards, R, C), mesh=mesh, in_specs=in_specs, out_specs=out_specs,
        check_vma=False,
    )
```

time: 33.2 us -> 29.2 us (0.88)
  Pallas kernels: 32.4 us -> 28.4 us
    pallas_call x1, Pallas kernels: 28.4 us -> 25.6 us  [shards(): pl.pallas_call(functools.partial(kernel, R, C), out_shape=(jax.ShapeDtype...]
    pallas_call x1, Pallas kernels: 3.99 us -> 2.83 us  [shards(): pl.pallas_call(finish, out_shape=(jax.ShapeDtypeStruct((H, nb, TB), jnp.f...]
where the time goes in v1:
time: 29.2 us; the launch traced here: 29.1 us
  Pallas kernels  28.4 us (97%)
  between operations  0.64 us (2%)
    pallas_call x1, Pallas kernels, shards(): pl.pallas_call(functools.partial(kernel, R, C), out_shape=(jax.ShapeDtype...  25.6 us
    pallas_call x1, Pallas kernels, shards(): pl.pallas_call(finish, out_shape=(jax.ShapeDtypeStruct((H, nb, TB), jnp.f...  2.83 us

profile of v1, /device:TPU:0, one launch (start us, length us, event | category | flops | bytes accessed | tf_op | source)
XLA Modules:
  0.0 29.1 jit_solution(3122999281875939563)
XLA Ops:
  0.6 25.6 %shard_map.76 = (f32[5,2,64]{2,1,0:T(2,128)S(1)}, f32[5,64,128]{2,1,0:T(8,128)S(1)}, f32[5,64,128]{2,1,0:T(8,128)S(1)}, f32[128,128]{1,0:T(8,128)S(1)}, f32[64,3...) custom-call(bf16[5,128,128]{2,1,0:T(8,128)(2,1)} %q_hbm.1, bf16[1024,128]{1,0:T(8,128)(2,1)} %k_hbm.1, s32[64]{0:T(128)} %doc_hbm.1, ...), custom_call_target="tpu_custom_call" | custom-call | tf_op jit(solution)/shard_map/pallas_call | solution.py:436
  26.2 2.8 %shard_map.77 = (f32[5,2,64]{2,1,0:T(2,128)}, f32[5,128,128]{2,1,0:T(8,128)}, f32[384,128]{1,0:T(8,128)}) custom-call(f32[5,2,64]{2,1,0:T(2,128)S(1)} %get-tuple-element.9.map_ref, f32[5,64,128]{2,1,0:T(8,128)S(1)} %get-tuple-element.10.qp_ref, f32[5,64,128]{2,1,0:T(8,128)S(1)} %get-tuple-element.11.qg_ref, f32[128,128]{1,0:T(8,128)S(1)} %get-tuple-element.12.both_ref, ...), custom_call_target="tpu_custom_call" | custom-call | tf_op jit(solution)/shard_map/pallas_call | solution.py:468

commit v2 on v1

--- a/solution.py
+++ b/solution.py
@@ -38,7 +38,7 @@
     R, C, q_hbm, k_hbm, doc_hbm, gq_hbm, gk_hbm,
     bm_ref, qp_ref, qg_ref, both_ref, pooled_ref, diff_ref,
     q_ref, gq_ref, gk_ref, doc_ref, kbuf, q_t, peak, bsum, kpool, pieces, diff_own, diff_all,
-    local, keysent, rsem, ps1, ps2, ps3, pctx, prow, ds1, dctx,
+    local, keysent, rsem, psem, ds1, dctx,
 ):
     H, rows, D = q_ref.shape
     shard = R * rows
@@ -107,6 +107,45 @@
     ]
     for load in loads:
         load.start()
+    pl.semaphore_wait(barrier, C - 1 + half)
+
+    def place(at, cc):
+        return jnp.where(at < cc, at, at - 1)
+
+    def copy_ctx(cc):
+        return pltpu.make_async_remote_copy(
+            src_ref=k_hbm.at[pl.ds(pl.multiple_of(r * rows, rows), rows)],
+            dst_ref=kbuf.at[chunk(c * R + r)],
+            send_sem=keysent.at[0], recv_sem=rsem.at[place(c, cc), 0],
+            device_id=(r, cc), device_id_type=MESH,
+        )
+
+    def copy_in(at, p, kind, to):
+        return pltpu.make_async_remote_copy(
+            src_ref=kbuf.at[at], dst_ref=kbuf.at[at],
+            send_sem=keysent.at[0], recv_sem=rsem.at[p, kind],
+            device_id=(to, c), device_id_type=MESH,
+        )
+
+    def arrived(p, kind, size):
+        at = kbuf.at[pl.ds(0, size)]
+        pltpu.make_async_copy(at, at, rsem.at[p, kind]).wait()
+
+    def copy_piece(at, kind, device):
+        return pltpu.make_async_remote_copy(
+            src_ref=pieces.at[at], dst_ref=pieces.at[at],
+            send_sem=psem.at[3], recv_sem=psem.at[kind],
+            device_id=device, device_id_type=MESH,
+        )
+
+    def pieces_arrived(kind, count):
+        at = kbuf.at[pl.ds(0, 2 * used * count)]
+        pltpu.make_async_copy(at, at, psem.at[kind]).wait()
+
+    @pl.loop(0, C - 1)
+    def _(i):
+        copy_ctx(far_first(i)).start()
+
     peak[...] = jnp.full_like(peak, NEG)
     bsum[...] = jnp.zeros_like(bsum)
     loads[0].wait()
@@ -117,71 +156,6 @@
             pieces[c, pl.ds(r * PIECE + h * nb + j, 1), :] = jnp.mean(
                 qf[j * BLK:(j + 1) * BLK], axis=0, keepdims=True
             )
-    pl.semaphore_wait(barrier, C - 1 + half)
-
-    def copy_ctx(cc):
-        return pltpu.make_async_remote_copy(
-            src_ref=k_hbm.at[pl.ds(pl.multiple_of(r * rows, rows), rows)],
-            dst_ref=kbuf.at[chunk(c * R + r)],
-            send_sem=keysent.at[0], recv_sem=rsem.at[c * R + r, 0],
-            device_id=(r, cc), device_id_type=MESH,
-        )
-
-    def copy_whole(num, to):
-        return pltpu.make_async_remote_copy(
-            src_ref=kbuf.at[chunk(num)], dst_ref=kbuf.at[chunk(num)],
-            send_sem=keysent.at[0], recv_sem=rsem.at[num, 0],
-            device_id=(to, c), device_id_type=MESH,
-        )
-
-    def copy_half(num, x, to):
-        return pltpu.make_async_remote_copy(
-            src_ref=kbuf.at[piece(num, x)], dst_ref=kbuf.at[piece(num, x)],
-            send_sem=keysent.at[0], recv_sem=rsem.at[num, x],
-            device_id=(to, c), device_id_type=MESH,
-        )
-
-    def arrived(num):
-        at = kbuf.at[chunk(num)]
-        pltpu.make_async_copy(at, at, rsem.at[num, 0]).wait()
-
-    def half_arrived(num, x):
-        at = kbuf.at[piece(num, x)]
-        pltpu.make_async_copy(at, at, rsem.at[num, x]).wait()
-
-    def piece1(d):
-        return pltpu.make_async_remote_copy(
-            src_ref=pieces.at[c, part(r)], dst_ref=pieces.at[c, part(r)],
-            send_sem=ps1.at[d], recv_sem=pctx.at[c],
-            device_id=(r, ctx_peer(d)), device_id_type=MESH,
-        )
-
-    def piece2(e):
-        return pltpu.make_async_remote_copy(
-            src_ref=pieces.at[:, part(r)], dst_ref=pieces.at[:, part(r)],
-            send_sem=ps2.at[e], recv_sem=prow.at[r],
-            device_id=(row_peer(e), c), device_id_type=MESH,
-        )
-
-    def piece3(e):
-        rr = row_peer(e)
-        return pltpu.make_async_remote_copy(
-            src_ref=pieces.at[:, part(rr)], dst_ref=pieces.at[:, part(rr)],
-            send_sem=ps3.at[e], recv_sem=prow.at[rr],
-            device_id=(partner, c), device_id_type=MESH,
-        )
-
-    def row_arrived(rr):
-        pltpu.make_async_copy(
-            pieces.at[:, part(rr)], pieces.at[:, part(rr)], prow.at[rr]
-        ).wait()
-
-    @pl.loop(0, C - 1)
-    def _(i):
-        copy_ctx(far_first(i)).start()
-
-    for d in range(1, C):
-        piece1(d).start()
 
     loads[2].wait()
     a0 = me * nb
@@ -225,8 +199,6 @@
         return (num + 1) * nb - 1 + most > a0
 
     def process(nums):
-        for num in nums:
-            pool(num)
         whole = (nums[0] < me) & near(nums[0])
         for num in nums[1:]:
             whole = whole & (num < me) & near(num)
@@ -247,88 +219,98 @@
 
     @pl.loop(0, half)
     def _(g):
+        pool(c * R + 2 * g)
+        pool(c * R + 2 * g + 1)
         process([c * R + 2 * g, c * R + 2 * g + 1])
-
-    @pl.loop(0, C - 1)
-    def _(i):
-        num = others(i) * R + r
-        arrived(num)
-        copy_half(num, 0, row_peer(1)).start()
-        copy_half(num, 1, row_peer(2)).start()
-        copy_half(num, 1, row_peer(1)).start()
-        copy_half(num, 0, row_peer(2)).start()
-        for e in range(4, half):
-            copy_whole(num, row_peer(e)).start()
-        copy_whole(num, partner).start()
-
-    @pl.loop(0, C - 1)
-    def _(i):
-        base = others(i) * R
-        half_arrived(base + row_peer(1), 0)
-        copy_half(base + row_peer(1), 0, row_peer(2)).start()
-        half_arrived(base + row_peer(2), 1)
-        copy_half(base + row_peer(2), 1, row_peer(1)).start()
-
-    for d in range(1, C):
-        cc = ctx_peer(d)
-        pltpu.make_async_copy(pieces.at[cc, part(r)], pieces.at[cc, part(r)], pctx.at[cc]).wait()
-    for e in range(1, half):
-        piece2(e).start()
-    piece3(0).start()
-
-    @pl.loop(0, C - 1)
-    def _(i):
-        base = others(i) * R
-        half_arrived(base + row_peer(1), 1)
-        copy_whole(base + row_peer(1), partner).start()
-        half_arrived(base + row_peer(2), 0)
-        copy_whole(base + row_peer(2), partner).start()
-
-    @pl.loop(0, C - 1)
-    def _(i):
-        base = others(i) * R
-        arrived(base + partner)
-        process([base + r, base + partner, base + row_peer(1), base + row_peer(2)])
-
-    @pl.loop(0, C - 1)
-    def _(i):
-        num = others(i) * R + row_peer(3)
-        half_arrived(num, 0)
-        half_arrived(num, 1)
-        copy_whole(num, partner).start()
-        for e in range(4, half):
-            arrived(others(i) * R + row_peer(e))
-            copy_whole(others(i) * R + row_peer(e), partner).start()
-
-    @pl.loop(0, C - 1)
-    def _(i):
-        base = others(i) * R
-        arrived(base + other_row(1))
-        arrived(base + other_row(2))
-        process([base + row_peer(3), base + other_row(1), base + other_row(2)])
-
-    for e in range(1, half):
-        row_arrived(row_peer(e))
-        piece3(e).start()
-
-    @pl.loop(0, C - 1)
-    def _(i):
-        base = others(i) * R
-        arrived(base + other_row(3))
-        process([base + other_row(3)])
-        for e in range(4, half):
-            arrived(base + other_row(e))
-            process([base + row_peer(e), base + other_row(e)])
 
     loads[3].wait()
     loads[4].wait()
-    pooled = jnp.concatenate([kpool[i] for i in range(3)], axis=1)
-    key_gate = gate(pooled, gk_ref[...])
     row16 = lax.broadcasted_iota(jnp.int32, (PIECE, 1), 0)
     own = jnp.where(row16 < used, pieces[c, pl.ds(pl.multiple_of(r * PIECE, PIECE), PIECE), :], 0.0)
     qg = jnp.zeros((PIECE, D), jnp.float32)
     for h in range(H):
         qg = jnp.where(row16 // nb == h, gate(own, gq_ref[h]), qg)
+
+    one, two, three = (row_peer(e) for e in (1, 2, 3))
+
+    @pl.loop(0, C - 1)
+    def _(i):
+        num = others(i) * R + r
+        arrived(i, 0, rows)
+        copy_in(piece(num, 0), i, 1, one).start()
+        copy_in(piece(num, 1), i, 2, two).start()
+        copy_in(piece(num, 1), i, 3, one).start()
+        copy_in(piece(num, 0), i, 3, two).start()
+        for e in range(4, half):
+            copy_in(chunk(num), i, 4 + e, row_peer(e)).start()
+        copy_in(chunk(num), i, 5, partner).start()
+        pool(num)
+
+    @pl.loop(0, C - 1)
+    def _(i):
+        base = others(i) * R
+        arrived(i, 1, cut)
+        copy_in(piece(base + one, 0), i, 4, two).start()
+        arrived(i, 2, cut)
+        copy_in(piece(base + two, 1), i, 4, one).start()
+
+    @pl.loop(0, C - 1)
+    def _(i):
+        base = others(i) * R
+        arrived(i, 3, rows)
+        copy_in(chunk(base + one), i, 6, partner).start()
+        copy_in(chunk(base + two), i, 6, partner).start()
+        pool(base + one)
+        pool(base + two)
+
+    for d in range(1, C):
+        copy_piece((c, part(r)), 0, (r, ctx_peer(d))).start()
+
+    @pl.loop(0, C - 1)
+    def _(i):
+        base = others(i) * R
+        arrived(i, 5, rows)
+        process([base + r, base + partner, base + one, base + two])
+
+    @pl.loop(0, C - 1)
+    def _(i):
+        num = others(i) * R + three
+        arrived(i, 4, rows)
+        copy_in(chunk(num), i, 7, partner).start()
+        for e in range(4, half):
+            far = others(i) * R + row_peer(e)
+            arrived(i, 4 + e, rows)
+            copy_in(chunk(far), i, half + e, partner).start()
+            pool(far)
+        pool(num)
+        pool(others(i) * R + partner)
+
+    pieces_arrived(0, C - 1)
+    for e in range(1, half):
+        copy_piece((slice(None), part(r)), 1, (row_peer(e), c)).start()
+    copy_piece((slice(None), part(r)), 2, (partner, c)).start()
+
+    @pl.loop(0, C - 1)
+    def _(i):
+        base = others(i) * R
+        arrived(i, 6, 2 * rows)
+        pool(base + other_row(1))
+        pool(base + other_row(2))
+        process([base + three, base + other_row(1), base + other_row(2)])
+
+    @pl.loop(0, C - 1)
+    def _(i):
+        base = others(i) * R
+        arrived(i, 7, rows)
+        pool(base + other_row(3))
+        process([base + other_row(3)])
+        for e in range(4, half):
+            arrived(i, half + e, rows)
+            pool(base + other_row(e))
+            process([base + row_peer(e), base + other_row(e)])
+
+    pooled = jnp.concatenate([kpool[i] for i in range(3)], axis=1)
+    key_gate = gate(pooled, gk_ref[...])
     logits = fdot(qg, key_gate, ((1,), (1,)))
 
     maps = jnp.full((PIECE, TB), NEG, jnp.float32)
@@ -370,8 +352,10 @@
         for j in range(nb):
             bm_ref[h, j:j + 1, :] = block_map[h * nb + j:h * nb + j + 1, :]
 
-    for e in range(half):
-        row_arrived(other_row(e))
+    pieces_arrived(1, (half - 1) * C)
+    for e in range(1, half):
+        copy_piece((slice(None), part(row_peer(e))), 2, (partner, c)).start()
+    pieces_arrived(2, half * C)
 
     def gathered(j):
         return jnp.concatenate(
@@ -392,12 +376,7 @@
     pltpu.make_async_copy(rest, rest, ds1.at[0]).wait()
     sent = kbuf.at[pl.ds(0, (C - 1) * shard)]
     pltpu.make_async_copy(sent, sent, keysent.at[0]).wait()
-    for d in range(1, C):
-        piece1(d).wait_send()
-    for e in range(half):
-        piece3(e).wait_send()
-        if e > 0:
-            piece2(e).wait_send()
+    pieces_arrived(3, n - 1)
 
 
 def finish(map_ref, qp_ref, qg_ref, both_ref, pooled_ref, diff_ref, bm_ref, dq_ref, dk_ref):
@@ -458,8 +437,7 @@
             pltpu.VMEM((C, R * PIECE, D), jnp.float32),
             pltpu.VMEM((H, nb * TB), jnp.float32),
             pltpu.VMEM((n, H, nb * TB), jnp.float32),
-            dma((5,)), dma((1,)), dma((n, 2)),
-            dma((C,)), dma((half,)), dma((half,)), dma((C,)), dma((R,)), dma((1,)), dma((1,)),
+            dma((5,)), dma((1,)), dma((C - 1, 2 * half)), dma((4,)), dma((1,)), dma((1,)),
         ],
         compiler_params=pltpu.CompilerParams(
             collective_id=0, has_side_effects=True, vmem_limit_bytes=VMEM_LIMIT

time: 29.2 us -> 28.1 us (0.962)
  Pallas kernels: 28.4 us -> 27.3 us
    pallas_call x1, Pallas kernels: 25.6 us -> 24.5 us  [shards(): pl.pallas_call(functools.partial(kernel, R, C), out_shape=(jax.ShapeDtype...]
where the time goes in v2:
time: 28.1 us; the launch traced here: 28 us
  Pallas kernels  27.3 us (97%)
  between operations  0.64 us (2%)
    pallas_call x1, Pallas kernels, shards(): pl.pallas_call(functools.partial(kernel, R, C), out_shape=(jax.ShapeDtype...  24.5 us
    pallas_call x1, Pallas kernels, shards(): pl.pallas_call(finish, out_shape=(jax.ShapeDtypeStruct((H, nb, TB), jnp.f...  2.83 us

profile of v2, /device:TPU:0, one launch (start us, length us, event | category | flops | bytes accessed | tf_op | source)
XLA Modules:
  0.0 28.0 jit_solution(14700215717304719583)
XLA Ops:
  0.6 24.5 %shard_map.76 = (f32[5,2,64]{2,1,0:T(2,128)S(1)}, f32[5,64,128]{2,1,0:T(8,128)S(1)}, f32[5,64,128]{2,1,0:T(8,128)S(1)}, f32[128,128]{1,0:T(8,128)S(1)}, f32[64,3...) custom-call(bf16[5,128,128]{2,1,0:T(8,128)(2,1)} %q_hbm.1, bf16[1024,128]{1,0:T(8,128)(2,1)} %k_hbm.1, s32[64]{0:T(128)} %doc_hbm.1, ...), custom_call_target="tpu_custom_call" | custom-call | tf_op jit(solution)/shard_map/pallas_call | solution.py:415
  25.1 2.8 %shard_map.77 = (f32[5,2,64]{2,1,0:T(2,128)}, f32[5,128,128]{2,1,0:T(8,128)}, f32[384,128]{1,0:T(8,128)}) custom-call(f32[5,2,64]{2,1,0:T(2,128)S(1)} %get-tuple-element.9.map_ref, f32[5,64,128]{2,1,0:T(8,128)S(1)} %get-tuple-element.10.qp_ref, f32[5,64,128]{2,1,0:T(8,128)S(1)} %get-tuple-element.11.qg_ref, f32[128,128]{1,0:T(8,128)S(1)} %get-tuple-element.12.both_ref, ...), custom_call_target="tpu_custom_call" | custom-call | tf_op jit(solution)/shard_map/pallas_call | solution.py:446

commit v3 on v2

--- a/solution.py
+++ b/solution.py
@@ -239,11 +239,15 @@
         arrived(i, 0, rows)
         copy_in(piece(num, 0), i, 1, one).start()
         copy_in(piece(num, 1), i, 2, two).start()
+        copy_in(chunk(num), i, 5, partner).start()
+
+    @pl.loop(0, C - 1)
+    def _(i):
+        num = others(i) * R + r
         copy_in(piece(num, 1), i, 3, one).start()
         copy_in(piece(num, 0), i, 3, two).start()
         for e in range(4, half):
             copy_in(chunk(num), i, 4 + e, row_peer(e)).start()
-        copy_in(chunk(num), i, 5, partner).start()
         pool(num)
 
     @pl.loop(0, C - 1)
@@ -364,39 +368,52 @@
 
     for h in range(H):
         qp = jnp.concatenate([gathered(h * nb + j) for j in range(nb)], axis=0)
-        qp_ref[h] = qp
-        qg_ref[h] = gate(qp, gq_ref[h])
-
+        qp_ref[h] = qp.T
+        qg = gate(qp, gq_ref[h])
+        for j in range(nb):
+            qg_ref[h * n:(h + 1) * n, j * D:(j + 1) * D] = qg[j * n:(j + 1) * n]
+
+    both_ref[...] = jnp.zeros_like(both_ref)
     for j in range(nb):
-        both_ref[j * TB:(j + 1) * TB] = key_gate
-    pooled_ref[...] = pooled
+        both_ref[j * TB:(j + 1) * TB, j * D:(j + 1) * D] = key_gate
+    for i in range(3):
+        pooled_ref[i * D:(i + 1) * D] = kpool[i].T
     rest = diff_all.at[pl.ds(0, n - 1)]
     pltpu.make_async_copy(rest, rest, dctx.at[0]).wait()
-    diff_ref[...] = diff_all[...]
+    for h in range(H):
+        diff_ref[h * n:(h + 1) * n] = diff_all[:, h, :]
     pltpu.make_async_copy(rest, rest, ds1.at[0]).wait()
     sent = kbuf.at[pl.ds(0, (C - 1) * shard)]
     pltpu.make_async_copy(sent, sent, keysent.at[0]).wait()
     pieces_arrived(3, n - 1)
 
 
-def finish(map_ref, qp_ref, qg_ref, both_ref, pooled_ref, diff_ref, bm_ref, dq_ref, dk_ref):
+def finish(
+    map_ref, qp_ref, qg_ref, both_ref, pooled_ref, diff_ref, bm_hbm, dq_hbm, dk_hbm,
+    dq_ref, dk_ref, sem,
+):
     H, nb, TB = map_ref.shape
-    bm_ref[...] = map_ref[...]
-    both = both_ref[...]
-    wide_lane = lax.broadcasted_iota(jnp.int32, (1, nb * TB), 1)
-    key_back = jnp.zeros(both.shape, jnp.float32)
-    for h in range(H):
-        mixed = diff_ref[:, h, :]
-        diff = jnp.concatenate(
-            [jnp.where(wide_lane // TB == j, mixed, 0.0) for j in range(nb)], axis=0
-        )
-        back = fdot(diff, both, ((1,), (0,)))
-        dq_ref[h] = fdot(qp_ref[h], back, ((0,), (0,)))
-        key_back = key_back + fdot(diff, qg_ref[h], ((0,), (0,)))
-    folded = key_back[:TB]
+    D = dq_ref.shape[-1]
+    n = diff_ref.shape[0] // H
+    out = pltpu.make_async_copy(map_ref, bm_hbm, sem.at[0])
+    out.start()
+    mixed = diff_ref[...]
+    spread = fdot(mixed, qg_ref[...], ((0,), (0,)))
+    folded = spread[:TB, :D]
     for j in range(1, nb):
-        folded = folded + key_back[j * TB:(j + 1) * TB]
-    dk_ref[...] = fdot(pooled_ref[...], folded, ((0,), (0,)))
+        folded = folded + spread[j * TB:(j + 1) * TB, j * D:(j + 1) * D]
+    back = fdot(mixed, both_ref[...], ((1,), (0,)))
+    dk_ref[...] = fdot(pooled_ref[...], folded, ((1,), (0,)))
+    keys_out = pltpu.make_async_copy(dk_ref, dk_hbm, sem.at[1])
+    keys_out.start()
+    for h in range(H):
+        rows = slice(h * n, (h + 1) * n)
+        own = jnp.concatenate([back[rows, j * D:(j + 1) * D] for j in range(nb)], axis=0)
+        dq_ref[h] = fdot(qp_ref[h], own, ((1,), (0,)))
+        pltpu.make_async_copy(dq_ref.at[h], dq_hbm.at[h], sem.at[2]).start()
+    out.wait()
+    keys_out.wait()
+    pltpu.make_async_copy(dq_ref, dq_hbm, sem.at[2]).wait()
 
 
 def shards(R, C, queries, keys, doc_ids, gate_query, gate_key):
@@ -416,11 +433,11 @@
         functools.partial(kernel, R, C),
         out_shape=(
             jax.ShapeDtypeStruct((H, nb, TB), jnp.float32),
-            jax.ShapeDtypeStruct((H, nb * n, D), jnp.float32),
-            jax.ShapeDtypeStruct((H, nb * n, D), jnp.float32),
-            jax.ShapeDtypeStruct((nb * TB, D), jnp.float32),
-            jax.ShapeDtypeStruct((TB, 3 * D), jnp.float32),
-            jax.ShapeDtypeStruct((n, H, nb * TB), jnp.float32),
+            jax.ShapeDtypeStruct((H, D, nb * n), jnp.float32),
+            jax.ShapeDtypeStruct((H * n, nb * D), jnp.float32),
+            jax.ShapeDtypeStruct((nb * TB, nb * D), jnp.float32),
+            jax.ShapeDtypeStruct((3 * D, TB), jnp.float32),
+            jax.ShapeDtypeStruct((H * n, nb * TB), jnp.float32),
         ),
         in_specs=[hbm] * 5,
         out_specs=(vm,) * 6,
@@ -451,7 +468,12 @@
             jax.ShapeDtypeStruct(gate_key.shape, jnp.float32),
         ),
         in_specs=[vm] * 6,
-        out_specs=(vm,) * 3,
+        out_specs=(hbm,) * 3,
+        scratch_shapes=[
+            pltpu.VMEM(gate_query.shape, jnp.float32),
+            pltpu.VMEM(gate_key.shape, jnp.float32),
+            dma((3,)),
+        ],
         compiler_params=pltpu.CompilerParams(vmem_limit_bytes=VMEM_LIMIT),
     )(*parts)
 

time: 28.1 us -> 26.9 us (0.957)
  Pallas kernels: 27.3 us -> 26.1 us
    pallas_call x1, Pallas kernels: 2.83 us -> 1.64 us  [shards(): pl.pallas_call(finish, out_shape=(jax.ShapeDtypeStruct((H, nb, TB), jnp.f...]
where the time goes in v3:
time: 26.9 us; the launch traced here: 26.7 us
  Pallas kernels  26.1 us (97%)
  between operations  0.64 us (2%)
    pallas_call x1, Pallas kernels, shards(): pl.pallas_call(functools.partial(kernel, R, C), out_shape=(jax.ShapeDtype...  24.4 us
    pallas_call x1, Pallas kernels, shards(): pl.pallas_call(finish, out_shape=(jax.ShapeDtypeStruct((H, nb, TB), jnp.f...  1.64 us

profile of v3, /device:TPU:0, one launch (start us, length us, event | category | flops | bytes accessed | tf_op | source)
XLA Modules:
  0.0 26.7 jit_solution(16599978909412507479)
XLA Ops:
  0.6 24.4 %shard_map.76 = (f32[5,2,64]{2,1,0:T(2,128)S(1)}, f32[5,128,64]{2,1,0:T(8,128)S(1)}, f32[160,256]{1,0:T(8,128)S(1)}, f32[128,256]{1,0:T(8,128)S(1)}, f32[384,64]{1,0:T(8,128)S(1)}, /*index=5*/f32[160,128]{1,0:T(8,128)S(1)}) custom-call(bf16[5,128,128]{2,1,0:T(8,128)(2,1)} %q_hbm.1, bf16[1024,128]{1,0:T(8,128)(2,1)} %k_hbm.1, s32[64]{0:T(128)} %doc_hbm.1, ...), custom_call_target="tpu_custom_call" | custom-call | tf_op jit(solution)/shard_map/pallas_call | solution.py:432
  25.1 1.6 %shard_map.77 = (f32[5,2,64]{2,1,0:T(2,128)}, f32[5,128,128]{2,1,0:T(8,128)}, f32[384,128]{1,0:T(8,128)}) custom-call(f32[5,2,64]{2,1,0:T(2,128)S(1)} %get-tuple-element.9.map_ref, f32[5,128,64]{2,1,0:T(8,128)S(1)} %get-tuple-element.10.qp_ref, f32[160,256]{1,0:T(8,128)S(1)} %get-tuple-element.11.qg_ref, f32[128,256]{1,0:T(8,128)S(1)} %get-tuple-element.12.both_ref, ...), custom_call_target="tpu_custom_call" | custom-call | tf_op jit(solution)/shard_map/pallas_call | solution.py:463

commit v4 on v3

--- a/solution.py
+++ b/solution.py
@@ -278,6 +278,14 @@
 
     @pl.loop(0, C - 1)
     def _(i):
+        base = others(i) * R
+        arrived(i, 6, 2 * rows)
+        pool(base + other_row(1))
+        pool(base + other_row(2))
+        process([base + other_row(1), base + other_row(2)])
+
+    @pl.loop(0, C - 1)
+    def _(i):
         num = others(i) * R + three
         arrived(i, 4, rows)
         copy_in(chunk(num), i, 7, partner).start()
@@ -296,11 +304,7 @@
 
     @pl.loop(0, C - 1)
     def _(i):
-        base = others(i) * R
-        arrived(i, 6, 2 * rows)
-        pool(base + other_row(1))
-        pool(base + other_row(2))
-        process([base + three, base + other_row(1), base + other_row(2)])
+        process([others(i) * R + three])
 
     @pl.loop(0, C - 1)
     def _(i):

time: 26.9 us -> 26.7 us (level)
  no operation moved by 1% of the time
where the time goes in v4:
time: 26.7 us; the launch traced here: 26.5 us
  Pallas kernels  25.9 us (97%)
  between operations  0.64 us (2%)
    pallas_call x1, Pallas kernels, shards(): pl.pallas_call(functools.partial(kernel, R, C), out_shape=(jax.ShapeDtype...  24.2 us
    pallas_call x1, Pallas kernels, shards(): pl.pallas_call(finish, out_shape=(jax.ShapeDtypeStruct((H, nb, TB), jnp.f...  1.64 us

profile of v4, /device:TPU:0, one launch (start us, length us, event | category | flops | bytes accessed | tf_op | source)
XLA Modules:
  0.0 26.5 jit_solution(6813929278259617304)
XLA Ops:
  0.6 24.2 %shard_map.76 = (f32[5,2,64]{2,1,0:T(2,128)S(1)}, f32[5,128,64]{2,1,0:T(8,128)S(1)}, f32[160,256]{1,0:T(8,128)S(1)}, f32[128,256]{1,0:T(8,128)S(1)}, f32[384,64]{1,0:T(8,128)S(1)}, /*index=5*/f32[160,128]{1,0:T(8,128)S(1)}) custom-call(bf16[5,128,128]{2,1,0:T(8,128)(2,1)} %q_hbm.1, bf16[1024,128]{1,0:T(8,128)(2,1)} %k_hbm.1, s32[64]{0:T(128)} %doc_hbm.1, ...), custom_call_target="tpu_custom_call" | custom-call | tf_op jit(solution)/shard_map/pallas_call | solution.py:436
  24.9 1.6 %shard_map.77 = (f32[5,2,64]{2,1,0:T(2,128)}, f32[5,128,128]{2,1,0:T(8,128)}, f32[384,128]{1,0:T(8,128)}) custom-call(f32[5,2,64]{2,1,0:T(2,128)S(1)} %get-tuple-element.9.map_ref, f32[5,128,64]{2,1,0:T(8,128)S(1)} %get-tuple-element.10.qp_ref, f32[160,256]{1,0:T(8,128)S(1)} %get-tuple-element.11.qg_ref, f32[128,256]{1,0:T(8,128)S(1)} %get-tuple-element.12.both_ref, ...), custom_call_target="tpu_custom_call" | custom-call | tf_op jit(solution)/shard_map/pallas_call | solution.py:467
